TPU v7x, 32 devices: a whole 2x2x4 slice. The times are simulated.
32 devices in a mesh: roll: 8 (over z, core), kvh: 4 (over y, x).
Axes of the slice: x: 2, y: 2, z: 4, core: 2. Of those that a mesh axis runs over, the one named last changes fastest.
Arguments:
- out_grad: bfloat16 [8, 256, 5120], P('roll', 'kvh'), may hold values from -48 to 48
- out_weight: bfloat16 [4, 5, 128, 5120], P('kvh'), may hold values from -0.078125 to 0.078125
- queries: bfloat16 [8, 256, 4, 5, 128], P('roll', None, 'kvh'), may hold values from -16 to 16
- keys_new: bfloat16 [8, 256, 4, 128], P('roll', None, 'kvh'), may hold values from -16 to 16
- values_new: bfloat16 [8, 256, 4, 128], P('roll', None, 'kvh'), may hold values from -6 to 6
- keys_prompt: bfloat16 [2048, 4, 128], P('roll', 'kvh'), may hold values from -6 to 6
- values_prompt: bfloat16 [2048, 4, 128], P('roll', 'kvh'), may hold values from -6 to 6
- offsets: int32 [8], P('roll'), may hold values from 0 to 3840
Outputs:
- grad_queries: bfloat16 [8, 256, 4, 5, 128], P('roll', None, 'kvh')
- grad_keys_new: bfloat16 [8, 256, 4, 128], P('roll', None, 'kvh')
- grad_values_new: bfloat16 [8, 256, 4, 128], P('roll', None, 'kvh')
- grad_keys_prompt: bfloat16 [2048, 4, 128], P('roll', 'kvh')
- grad_values_prompt: bfloat16 [2048, 4, 128], P('roll', 'kvh')
Inputs may be any that keep to these rules, and one draw needn't show every extreme that they name: `offsets`: each slice lies inside a response of 4096 tokens.
All inputs are finite; a program needn't handle non-finite values.
Results may differ from a plain program's by a relative error of at most 0.015.
The roundings to bfloat16 on the way count: a program that leaves them out, or rounds other values in their place, can miss the bound.
Values may be sent and summed in bfloat16 or wider, within the bound.
No kernel may reach another device: no remote copies, remote signals or barrier semaphores. Data moves between devices by JAX's collectives and lax.ppermute only.
A program may use at most 64 MiB of HBM per device.

v0:
```python
import math
import jax
import jax.numpy as jnp
from jax import lax
from jax.sharding import PartitionSpec as P

theta_base = 1000000.0


def rotation(positions, head_width):
    half_width = head_width // 2
    frequency = jnp.power(theta_base, -(jnp.arange(half_width, dtype=jnp.float32) / half_width))
    angles = positions.astype(jnp.float32)[:, None] * frequency[None, :]
    return (jnp.cos(angles), jnp.sin(angles))


def rotate(vectors, cos_part, sin_part, direction):
    half_width = vectors.shape[-1] // 2
    front_half = vectors[..., :half_width]
    back_half = vectors[..., half_width:]
    return jnp.concatenate(
        [
            front_half * cos_part - direction * back_half * sin_part,
            back_half * cos_part + direction * front_half * sin_part,
        ],
        axis=-1,
    )


def inner_dot(left, right):
    return lax.dot_general(
        left, right, (((1,), (1,)), ((), ())), preferred_element_type=jnp.float32
    )


def outer_sum(left, right):
    return lax.dot_general(
        left, right, (((0,), (0,)), ((), ())), preferred_element_type=jnp.float32
    )


def block_grads(context, key_block, value_block):
    query_rows, grad_rows, log_total, row_delta, score_scale = context
    scores = inner_dot(query_rows, key_block) * score_scale
    attn_probs = jnp.exp(scores - log_total[:, None]).astype(jnp.bfloat16)
    prob_grad = inner_dot(grad_rows, value_block)
    score_grad = (
        attn_probs.astype(jnp.float32) * (prob_grad - row_delta[:, None]) * score_scale
    ).astype(jnp.bfloat16)
    return (attn_probs, score_grad)


def prompt_terms(context, key_rows, value_rows):
    row_count, head_width = key_rows.shape
    block_len = math.gcd(row_count, 512)
    key_blocks = key_rows.reshape(row_count // block_len, block_len, head_width)
    value_blocks = value_rows.reshape(row_count // block_len, block_len, head_width)

    def term_step(unused, blocks):
        attn_probs, score_grad = block_grads(context, blocks[0], blocks[1])
        return (
            unused,
            jnp.stack(
                [outer_sum(score_grad, context[0]), outer_sum(attn_probs, context[1])], axis=1
            ),
        )

    unused, block_terms = lax.scan(
        term_step, jnp.zeros((), jnp.float32), (key_blocks, value_blocks)
    )
    return block_terms.reshape(row_count, 2, head_width)


def local(out_grad, out_weight, queries, keys_new, values_new, keys_prompt, values_prompt, offsets):
    roll_local, seq_len, kv_local, group_size, head_width = queries.shape
    prompt_local = keys_prompt.shape[0]
    prompt_total = prompt_local * lax.axis_size("roll")
    score_scale = head_width ** (-0.5)
    row_total = roll_local * seq_len * group_size
    attn_grad = jnp.einsum(
        "rsc,ghdc->rsghd",
        lax.all_gather(out_grad, "kvh", axis=1, tiled=True),
        out_weight,
        preferred_element_type=jnp.float32,
    ).astype(jnp.bfloat16)
    cached_keys, cached_values = (
        lax.all_gather(keys_prompt, "roll", axis=0, tiled=True),
        lax.all_gather(values_prompt, "roll", axis=0, tiled=True),
    )
    positions = prompt_total + offsets[:, None] + jnp.arange(seq_len, dtype=jnp.int32)[None, :]
    cos_flat, sin_flat = rotation(positions.reshape(-1), head_width)
    cos_four = cos_flat.reshape(roll_local, seq_len, 1, head_width // 2)
    sin_four = sin_flat.reshape(roll_local, seq_len, 1, head_width // 2)
    query_rot = rotate(
        queries.astype(jnp.float32), cos_four[:, :, :, None], sin_four[:, :, :, None], 1.0
    ).astype(jnp.bfloat16)
    key_rot = rotate(keys_new.astype(jnp.float32), cos_four, sin_four, 1.0).astype(jnp.bfloat16)
    block_len = math.gcd(prompt_total, 512)
    block_count = prompt_total // block_len
    causal = (jnp.arange(seq_len)[None, :] <= jnp.arange(seq_len)[:, None])[None, :, None, :]
    head_index = 0
    query_head = query_rot[:, :, head_index]
    key_head = key_rot[:, :, head_index]
    value_head = values_new[:, :, head_index]
    grad_head = attn_grad[:, :, head_index]
    query_rows = query_head.reshape(row_total, head_width)
    grad_rows = grad_head.reshape(row_total, head_width)
    key_blocks = cached_keys[:, head_index].reshape(block_count, block_len, head_width)
    value_blocks = cached_values[:, head_index].reshape(block_count, block_len, head_width)
    near_scores = (
        jnp.einsum("rshd,rtd->rsht", query_head, key_head, preferred_element_type=jnp.float32)
        * score_scale
    )
    near_scores = jnp.where(causal, near_scores, -jnp.inf)
    near_max = jnp.max(near_scores, axis=3, keepdims=True)
    near_sum = jnp.sum(jnp.exp(near_scores - near_max), axis=3)

    def stat_step(running, key_block):
        old_max, old_sum = running
        scores = inner_dot(query_rows, key_block) * score_scale
        new_max = jnp.maximum(old_max, jnp.max(scores, axis=1))
        new_sum = old_sum * jnp.exp(old_max - new_max) + jnp.sum(
            jnp.exp(scores - new_max[:, None]), axis=1
        )
        return ((new_max, new_sum), None)

    stats, unused = lax.scan(
        stat_step, (near_max.reshape(row_total), near_sum.reshape(row_total)), key_blocks
    )
    log_total = stats[0] + jnp.log(stats[1])
    log_shaped = log_total.reshape(roll_local, seq_len, group_size, 1)
    near_probs = jnp.where(causal, jnp.exp(near_scores - log_shaped), 0.0).astype(jnp.bfloat16)
    near_output = jnp.einsum(
        "rsht,rtd->rshd", near_probs, value_head, preferred_element_type=jnp.float32
    ).reshape(row_total, head_width)

    def output_step(total_out, blocks):
        scores = inner_dot(query_rows, blocks[0]) * score_scale
        attn_probs = jnp.exp(scores - log_total[:, None]).astype(jnp.bfloat16)
        return (
            total_out + jnp.dot(attn_probs, blocks[1], preferred_element_type=jnp.float32),
            None,
        )

    output, unused = lax.scan(output_step, near_output, (key_blocks, value_blocks))
    row_delta = jnp.sum(grad_rows.astype(jnp.float32) * output, axis=1)
    context = (query_rows, grad_rows, log_total, row_delta, score_scale)
    contexts = [context]
    near_prob_grad = jnp.einsum(
        "rshd,rtd->rsht", grad_head, value_head, preferred_element_type=jnp.float32
    )
    delta_shaped = row_delta.reshape(roll_local, seq_len, group_size, 1)
    near_grad = (
        near_probs.astype(jnp.float32) * (near_prob_grad - delta_shaped) * score_scale
    ).astype(jnp.bfloat16)
    near_query = jnp.einsum(
        "rsht,rtd->rshd", near_grad, key_head, preferred_element_type=jnp.float32
    )
    key_new_grad = jnp.einsum(
        "rsht,rshd->rtd", near_grad, query_head, preferred_element_type=jnp.float32
    )
    value_new_grad = jnp.einsum(
        "rsht,rshd->rtd", near_probs, grad_head, preferred_element_type=jnp.float32
    )
    zero_rows = jnp.zeros((row_total, head_width), jnp.float32)

    def query_step(total_grad, blocks):
        attn_probs, score_grad = block_grads(context, blocks[0], blocks[1])
        return (
            total_grad + jnp.dot(score_grad, blocks[0], preferred_element_type=jnp.float32),
            None,
        )

    far_query, unused = lax.scan(query_step, zero_rows, (key_blocks, value_blocks))
    query_grad = far_query.reshape(roll_local, seq_len, group_size, head_width) + near_query
    query_list = [rotate(query_grad, cos_four, sin_four, -1.0).astype(jnp.bfloat16)]
    key_list = [
        rotate(key_new_grad, cos_four[:, :, 0], sin_four[:, :, 0], -1.0).astype(jnp.bfloat16)
    ]
    value_list = [value_new_grad.astype(jnp.bfloat16)]
    head_index = 0
    key_rows = cached_keys[:, head_index]
    value_rows = cached_values[:, head_index]
    pieces = [prompt_terms(contexts[head_index], key_rows, value_rows)]
    reduced = lax.psum_scatter(
        jnp.stack(pieces, axis=1).astype(jnp.bfloat16), "roll", scatter_dimension=0, tiled=True
    ).astype(jnp.float32)
    grad_queries = jnp.stack(query_list, axis=2)
    grad_keys_new = jnp.stack(key_list, axis=2)
    grad_values_new = jnp.stack(value_list, axis=2)
    return (
        grad_queries,
        grad_keys_new,
        grad_values_new,
        reduced[:, :, 0].astype(jnp.bfloat16),
        reduced[:, :, 1].astype(jnp.bfloat16),
    )


def solution(mesh):
    placed = (
        P("roll", "kvh", None),
        P("kvh", None, None, None),
        P("roll", None, "kvh", None, None),
        P("roll", None, "kvh", None),
        P("roll", None, "kvh", None),
        P("roll", "kvh", None),
        P("roll", "kvh", None),
        P("roll"),
    )
    return jax.shard_map(
        local,
        mesh=mesh,
        in_specs=placed,
        out_specs=(
            P("roll", None, "kvh", None, None),
            P("roll", None, "kvh", None),
            P("roll", None, "kvh", None),
            P("roll", "kvh", None),
            P("roll", "kvh", None),
        ),
        check_vma=False,
    )
```

profile of v0, /device:TPU:0, one launch (start us, length us, event | category | flops | bytes accessed | tf_op | source)
XLA Modules:
  0.0 133.3 jit_solution(5835152332438345986)
XLA Ops:
  8.0 17.7 %all_gather.9 = bf16[2048,1,128]{2,0,1:T(8,128)(2,1)} all-gather(bf16[256,1,128]{2,0,1:T(8,128)(2,1)} %param.21), channel_id=1, replica_groups=mesh['roll'=8,'kvh'=4] {'roll'}, dimensions={0}, use_global_device_ids=true | all-gather | bytes 589824 | tf_op jit(solution)/shard_map/all_gather | solution.py:87
  32.4 7.5 %while.43 = (s32[]{:T(128)}, f32[1280]{0:T(1024)S(1)}, f32[1280]{0:T(1024)S(1)}, bf16[4,512,128]{2,1,0:T(8,128)(2,1)}, bf16[1280,128]{1,0:T(8,128)(2,1)S(1)}, /*index=5*/s32[]{:T(128)}) while((s32[]{:T(128)}, f32[1280]{0:T(1024)S(1)}, f32[1280]{0:T(1024)S(1)}, bf16[4,512,128]{2,1,0:T(8,128)(2,1)}, bf16[1280,128]{1,0:T(8,128)(2,1)S(1)}, ...), condition=%wide.region_5.6_spmd, body=%wide.region_2.5_spmd.sunk | while | flops 170396160 | bytes 5768273 | solution.py:127
  42.1 16.1 %all_gather.10 = bf16[2048,1,128]{2,0,1:T(8,128)(2,1)} all-gather(bf16[256,1,128]{2,0,1:T(8,128)(2,1)S(1)} %copy-done.14), channel_id=1, replica_groups=mesh['roll'=8,'kvh'=4] {'roll'}, dimensions={0}, use_global_device_ids=true | all-gather | bytes 589824 | tf_op jit(solution)/shard_map/all_gather | solution.py:88
  58.6 7.8 %while.44 = (s32[]{:T(128)}, f32[1280,128]{1,0:T(8,128)S(1)}, bf16[4,512,128]{2,1,0:T(8,128)(2,1)}, bf16[1280,128]{1,0:T(8,128)(2,1)S(1)}, f32[1280]{0:T(1024)S(1)}, /*index=5*/bf16[4,512,128]{2,1,0:T(8,128)(2,1)}, s32[]{:T(128)}) while((s32[]{:T(128)}, f32[1280,128]{1,0:T(8,128)S(1)}, bf16[4,512,128]{2,1,0:T(8,128)(2,1)}, ...), condition=%wide.region_7.8_spmd, body=%wide.region_6.7_spmd.sunk | while | flops 337674240 | bytes 1906773 | solution.py:145
  58.6 1.9 %convolution_add_fusion.5 = f32[1280,128]{1,0:T(8,128)S(1)} fusion(f32[1280,128]{1,0:T(8,128)S(1)} %get-tuple-element.468, bf16[1280,128]{1,0:T(8,128)(2,1)S(1)} %get-tuple-element.477, f32[1280]{0:T(1024)S(1)} %get-tuple-element.478, bf16[4,512,128]{2,1,0:T(8,128)(2,1)} %get-tuple-element.479, s32[]{:T(128)S(6)} %copy.87, ...), kind=kOutput, calls=%fused_computation.10.clone.1 | convolution fusion | flops 337674240 | bytes 1906688 | tf_op jit(solution)/shard_map/while/body/eval_jaxpr/dot_general | solution.py:141
  60.5 1.9 %convolution_add_fusion.5 = f32[1280,128]{1,0:T(8,128)S(1)} fusion(f32[1280,128]{1,0:T(8,128)S(1)} %get-tuple-element.468, bf16[1280,128]{1,0:T(8,128)(2,1)S(1)} %get-tuple-element.477, f32[1280]{0:T(1024)S(1)} %get-tuple-element.478, bf16[4,512,128]{2,1,0:T(8,128)(2,1)} %get-tuple-element.479, s32[]{:T(128)S(6)} %copy.87, ...), kind=kOutput, calls=%fused_computation.10.clone.1 | convolution fusion | flops 337674240 | bytes 1906688 | tf_op jit(solution)/shard_map/while/body/eval_jaxpr/dot_general | solution.py:141
  62.5 1.9 %convolution_add_fusion.5 = f32[1280,128]{1,0:T(8,128)S(1)} fusion(f32[1280,128]{1,0:T(8,128)S(1)} %get-tuple-element.468, bf16[1280,128]{1,0:T(8,128)(2,1)S(1)} %get-tuple-element.477, f32[1280]{0:T(1024)S(1)} %get-tuple-element.478, bf16[4,512,128]{2,1,0:T(8,128)(2,1)} %get-tuple-element.479, s32[]{:T(128)S(6)} %copy.87, ...), kind=kOutput, calls=%fused_computation.10.clone.1 | convolution fusion | flops 337674240 | bytes 1906688 | tf_op jit(solution)/shard_map/while/body/eval_jaxpr/dot_general | solution.py:141
  64.4 1.9 %convolution_add_fusion.5 = f32[1280,128]{1,0:T(8,128)S(1)} fusion(f32[1280,128]{1,0:T(8,128)S(1)} %get-tuple-element.468, bf16[1280,128]{1,0:T(8,128)(2,1)S(1)} %get-tuple-element.477, f32[1280]{0:T(1024)S(1)} %get-tuple-element.478, bf16[4,512,128]{2,1,0:T(8,128)(2,1)} %get-tuple-element.479, s32[]{:T(128)S(6)} %copy.87, ...), kind=kOutput, calls=%fused_computation.10.clone.1 | convolution fusion | flops 337674240 | bytes 1906688 | tf_op jit(solution)/shard_map/while/body/eval_jaxpr/dot_general | solution.py:141
  66.4 5.9 %fusion.67 = bf16[256,5,128]{2,0,1:T(8,128)(2,1)S(1)} fusion(bf16[1,5,128,5120]{3,2,1,0:T(8,128)(2,1)} %param.17, bf16[1,256,5120]{2,1,0:T(8,128)(2,1)} %all-gather.2.cloned.1.call-done), kind=kOutput, calls=%fused_computation.75 | convolution fusion | flops 1677885440 | bytes 9502720 | tf_op jit(solution)/shard_map/rsc,ghdc->rsghd/dot_general | solution.py:80
  74.2 15.7 %while.45 = (s32[]{:T(128)}, bf16[4,512,2,128]{3,1,2,0:T(8,128)(2,1)S(1)}, bf16[4,512,128]{2,1,0:T(8,128)(2,1)}, bf16[1280,128]{1,0:T(8,128)(2,1)S(1)}, f32[1280...) while((s32[]{:T(128)}, ...), condition=%wide.region_12.13_spmd, body=%wide.region_11.12_spmd.sunk | while | flops 676855808 | bytes 6301809 | solution.py:68
  76.2 1.9 %fusion.153 = bf16[512,1,128]{2,0,1:T(8,128)(2,1)S(1)} fusion(bf16[1280,128]{1,0:T(8,128)(2,1)S(1)} %get-tuple-element.532, bf16[1280,128]{1,0:T(8,128)(2,1)S(1)} %get-tuple-element.535, bf16[512,1280]{1,0:T(8,128)(2,1)S(1)} %fusion.152, f32[1280]{0:T(1024)S(1)} %get-tuple-element.536, bf16[4,512,128]{2,1,0:T(8,128)(2,1)} %get-tuple-element.534, ...), kind=kOutput, calls=%fused_computation.30.clone.1 | convolution fusion | flops 338821120 | bytes 2233348 | tf_op jit(solution)/shard_map/while/body/eval_jaxpr/dot_general | solution.py:37
  78.2 1.5 %fusion.152 = bf16[512,1280]{1,0:T(8,128)(2,1)S(1)} fusion(bf16[1280,128]{1,0:T(8,128)(2,1)S(1)} %get-tuple-element.532, f32[1280]{0:T(1024)S(1)} %get-tuple-element.533, bf16[4,512,128]{2,1,0:T(8,128)(2,1)} %get-tuple-element.531, s32[]{:T(128)S(6)} %copy.99), kind=kOutput, calls=%fused_computation.25.clone.1 | convolution fusion | flops 169738240 | bytes 1774596 | tf_op jit(solution)/shard_map/while/body/eval_jaxpr/dot_general | solution.py:31
  80.2 1.9 %fusion.153 = bf16[512,1,128]{2,0,1:T(8,128)(2,1)S(1)} fusion(bf16[1280,128]{1,0:T(8,128)(2,1)S(1)} %get-tuple-element.532, bf16[1280,128]{1,0:T(8,128)(2,1)S(1)} %get-tuple-element.535, bf16[512,1280]{1,0:T(8,128)(2,1)S(1)} %fusion.152, f32[1280]{0:T(1024)S(1)} %get-tuple-element.536, bf16[4,512,128]{2,1,0:T(8,128)(2,1)} %get-tuple-element.534, ...), kind=kOutput, calls=%fused_computation.30.clone.1 | convolution fusion | flops 338821120 | bytes 2233348 | tf_op jit(solution)/shard_map/while/body/eval_jaxpr/dot_general | solution.py:37
  82.1 1.5 %fusion.152 = bf16[512,1280]{1,0:T(8,128)(2,1)S(1)} fusion(bf16[1280,128]{1,0:T(8,128)(2,1)S(1)} %get-tuple-element.532, f32[1280]{0:T(1024)S(1)} %get-tuple-element.533, bf16[4,512,128]{2,1,0:T(8,128)(2,1)} %get-tuple-element.531, s32[]{:T(128)S(6)} %copy.99), kind=kOutput, calls=%fused_computation.25.clone.1 | convolution fusion | flops 169738240 | bytes 1774596 | tf_op jit(solution)/shard_map/while/body/eval_jaxpr/dot_general | solution.py:31
  84.1 1.9 %fusion.153 = bf16[512,1,128]{2,0,1:T(8,128)(2,1)S(1)} fusion(bf16[1280,128]{1,0:T(8,128)(2,1)S(1)} %get-tuple-element.532, bf16[1280,128]{1,0:T(8,128)(2,1)S(1)} %get-tuple-element.535, bf16[512,1280]{1,0:T(8,128)(2,1)S(1)} %fusion.152, f32[1280]{0:T(1024)S(1)} %get-tuple-element.536, bf16[4,512,128]{2,1,0:T(8,128)(2,1)} %get-tuple-element.534, ...), kind=kOutput, calls=%fused_computation.30.clone.1 | convolution fusion | flops 338821120 | bytes 2233348 | tf_op jit(solution)/shard_map/while/body/eval_jaxpr/dot_general | solution.py:37
  86.1 1.5 %fusion.152 = bf16[512,1280]{1,0:T(8,128)(2,1)S(1)} fusion(bf16[1280,128]{1,0:T(8,128)(2,1)S(1)} %get-tuple-element.532, f32[1280]{0:T(1024)S(1)} %get-tuple-element.533, bf16[4,512,128]{2,1,0:T(8,128)(2,1)} %get-tuple-element.531, s32[]{:T(128)S(6)} %copy.99), kind=kOutput, calls=%fused_computation.25.clone.1 | convolution fusion | flops 169738240 | bytes 1774596 | tf_op jit(solution)/shard_map/while/body/eval_jaxpr/dot_general | solution.py:31
  88.1 1.9 %fusion.153 = bf16[512,1,128]{2,0,1:T(8,128)(2,1)S(1)} fusion(bf16[1280,128]{1,0:T(8,128)(2,1)S(1)} %get-tuple-element.532, bf16[1280,128]{1,0:T(8,128)(2,1)S(1)} %get-tuple-element.535, bf16[512,1280]{1,0:T(8,128)(2,1)S(1)} %fusion.152, f32[1280]{0:T(1024)S(1)} %get-tuple-element.536, bf16[4,512,128]{2,1,0:T(8,128)(2,1)} %get-tuple-element.534, ...), kind=kOutput, calls=%fused_computation.30.clone.1 | convolution fusion | flops 338821120 | bytes 2233348 | tf_op jit(solution)/shard_map/while/body/eval_jaxpr/dot_general | solution.py:37
  91.1 17.3 %while.46 = (s32[]{:T(128)}, f32[1280,128]{1,0:T(8,128)}, bf16[4,512,128]{2,1,0:T(8,128)(2,1)}, bf16[1280,128]{1,0:T(8,128)(2,1)S(1)}, f32[1280]{0:T(1024)S(1)},...) while((s32[]{:T(128)}, f32[1280,128]{1,0:T(8,128)}, ...), condition=%wide.region_10.11_spmd.clone, body=%wide.region_9.10_spmd.clone.sunk | while | flops 508887040 | bytes 7614074 | solution.py:174
  92.5 2.7 %convolution_add_fusion.6 = f32[1280,128]{1,0:T(8,128)} fusion(f32[512,1280]{1,0:T(8,128)S(1)} %fusion.160, bf16[1280,128]{1,0:T(8,128)(2,1)S(1)} %get-tuple-element.507, f32[1280]{0:T(1024)S(1)} %get-tuple-element.508, f32[1280,128]{1,0:T(8,128)} %get-tuple-element.492, pred[]{:T(512)S(6)} %compare.3, bf16[4,512,128]{2,1,0:T(8,128)(2,1)} %get-tuple-element.506, ...), kind=kOutput, calls=%fused_computation.50.clone.1 | convolution fusion | flops 338493440 | bytes 4528640 | tf_op jit(solution)/shard_map/while/body/eval_jaxpr/dot_general | solution.py:170
  96.6 2.9 %convolution_add_fusion.6 = f32[1280,128]{1,0:T(8,128)} fusion(f32[512,1280]{1,0:T(8,128)S(1)} %fusion.160, bf16[1280,128]{1,0:T(8,128)(2,1)S(1)} %get-tuple-element.507, f32[1280]{0:T(1024)S(1)} %get-tuple-element.508, f32[1280,128]{1,0:T(8,128)} %get-tuple-element.492, pred[]{:T(512)S(6)} %compare.3, bf16[4,512,128]{2,1,0:T(8,128)(2,1)} %get-tuple-element.506, ...), kind=kOutput, calls=%fused_computation.50.clone.1 | convolution fusion | flops 338493440 | bytes 4528640 | tf_op jit(solution)/shard_map/while/body/eval_jaxpr/dot_general | solution.py:170
  101.0 2.9 %convolution_add_fusion.6 = f32[1280,128]{1,0:T(8,128)} fusion(f32[512,1280]{1,0:T(8,128)S(1)} %fusion.160, bf16[1280,128]{1,0:T(8,128)(2,1)S(1)} %get-tuple-element.507, f32[1280]{0:T(1024)S(1)} %get-tuple-element.508, f32[1280,128]{1,0:T(8,128)} %get-tuple-element.492, pred[]{:T(512)S(6)} %compare.3, bf16[4,512,128]{2,1,0:T(8,128)(2,1)} %get-tuple-element.506, ...), kind=kOutput, calls=%fused_computation.50.clone.1 | convolution fusion | flops 338493440 | bytes 4528640 | tf_op jit(solution)/shard_map/while/body/eval_jaxpr/dot_general | solution.py:170
  105.4 2.9 %convolution_add_fusion.6 = f32[1280,128]{1,0:T(8,128)} fusion(f32[512,1280]{1,0:T(8,128)S(1)} %fusion.160, bf16[1280,128]{1,0:T(8,128)(2,1)S(1)} %get-tuple-element.507, f32[1280]{0:T(1024)S(1)} %get-tuple-element.508, f32[1280,128]{1,0:T(8,128)} %get-tuple-element.492, pred[]{:T(512)S(6)} %compare.3, bf16[4,512,128]{2,1,0:T(8,128)(2,1)} %get-tuple-element.506, ...), kind=kOutput, calls=%fused_computation.50.clone.1 | convolution fusion | flops 338493440 | bytes 4528640 | tf_op jit(solution)/shard_map/while/body/eval_jaxpr/dot_general | solution.py:170
  114.7 10.2 %reduce-scatter.2.cloned.1.call-done = bf16[256,1,2,128]{3,0,2,1:T(8,128)(2,1)} async-done(((bf16[2048,1,2,128]{3,0,2,1:T(8,128)(2,1)}), bf16[256,1,2,128]{3,0,2,1:T(8,128)(2,1)}) %reduce-scatter.2.cloned.1.call-update) | async-done | bytes 131088 | tf_op jit(solution)/shard_map/reduce_scatter | solution.py:185
  124.9 1.5 %slice_bitcast_fusion = (bf16[256,1,128]{2,0,1:T(8,128)(2,1)}, bf16[256,1,128]{2,0,1:T(8,128)(2,1)}) fusion(bf16[256,1,2,128]{3,0,2,1:T(8,128)(2,1)} %reduce-scatter.2.cloned.1.call-done), kind=kLoop, calls=%fused_computation.113 | loop fusion | bytes 262144 | tf_op jit(solution)/shard_map/convert_element_type | solution.py:196
  (116 shorter events, 35.1 us)
Async XLA Ops:
  7.2 51.1 %copy-start = (bf16[1,256,1,128]{3,1,2,0:T(8,128)(2,1)S(1)}, bf16[1,256,1,128]{3,1,2,0:T(8,128)(2,1)}, u32[]{:S(2)}) copy-start(bf16[1,256,1,128]{3,1,2,0:T(8,128)(2,1)} %param.20) | copy-start | bytes 196612
  7.2 59.2 %all-gather.2.cloned.1.call-start = ((), (), s32[]{:S(2)}) async-start(), calls=%async_computation.1 | async-start | bytes 3276800 | tf_op jit(solution)/shard_map/all_gather | solution.py:82
  7.9 117.0 %reduce-scatter.2.cloned.1.call-start = ((), (), s32[]{:S(2)}) async-start(), calls=%async_computation.2 | async-start | bytes 1179648 | tf_op jit(solution)/shard_map/reduce_scatter | solution.py:185
  28.6 1.3 copy-start.13
  28.9 2.1 %copy-start.3 = (bf16[1,256,1,5,64]{4,1,3,2,0:T(8,128)(2,1)}, bf16[1,256,1,5,64]{4,1,3,2,0:T(8,128)(2,1)S(1)}, u32[]{:S(2)}) copy-start(bf16[1,256,1,5,64]{4,1,3,2,0:T(8,128)(2,1)S(1)} %get-tuple-element.257) | copy-start | bytes 491524
  28.9 2.1 %copy-start.5 = (bf16[1,256,1,5,64]{4,1,3,2,0:T(8,128)(2,1)}, bf16[1,256,1,5,64]{4,1,3,2,0:T(8,128)(2,1)S(1)}, u32[]{:S(2)}) copy-start(bf16[1,256,1,5,64]{4,1,3,2,0:T(8,128)(2,1)S(1)} %get-tuple-element.258) | copy-start | bytes 491524
  30.5 1.6 %copy-start.10 = (bf16[256,64]{1,0:T(8,128)(2,1)}, bf16[256,64]{1,0:T(8,128)(2,1)S(1)}, u32[]{:S(2)}) copy-start(bf16[256,64]{1,0:T(8,128)(2,1)S(1)} %get-tuple-element.264) | copy-start | bytes 98308
  40.3 1.9 %copy-start.14 = (bf16[256,1,128]{2,0,1:T(8,128)(2,1)S(1)}, bf16[256,1,128]{2,0,1:T(8,128)(2,1)}, u32[]{:S(2)}) copy-start(bf16[256,1,128]{2,0,1:T(8,128)(2,1)} %param.22) | copy-start | bytes 196612
  40.6 0.9 copy-start.1
  72.3 0.7 copy-start.7
  73.0 1.2 copy-start.9
  108.3 1.9 %copy-start.2 = (bf16[256,5,256]{2,0,1:T(8,128)(2,1)S(1)}, bf16[256,5,256]{2,0,1:T(8,128)(2,1)}, u32[]{:S(2)}) copy-start(bf16[256,5,256]{2,0,1:T(8,128)(2,1)} %copy-done.1) | copy-start | bytes 1966084
  108.3 1.9 %copy-start.8 = (bf16[256,5,128]{2,0,1:T(8,128)(2,1)S(1)}, bf16[256,5,128]{2,0,1:T(8,128)(2,1)}, u32[]{:S(2)}) copy-start(bf16[256,5,128]{2,0,1:T(8,128)(2,1)} %copy-done.7) | copy-start | bytes 983044
  108.5 2.1 %copy-start.11 = (bf16[256,64]{1,0:T(8,128)(2,1)S(1)}, bf16[256,64]{1,0:T(8,128)(2,1)}, u32[]{:S(2)}) copy-start(bf16[256,64]{1,0:T(8,128)(2,1)} %copy-done.10) | copy-start | bytes 98308
  109.8 1.3 copy-start.12
  110.6 1.5 %copy-start.4 = (bf16[1,256,1,5,64]{4,1,3,2,0:T(8,128)(2,1)S(1)}, bf16[1,256,1,5,64]{4,1,3,2,0:T(8,128)(2,1)}, u32[]{:S(2)}) copy-start(bf16[1,256,1,5,64]{4,1,3,2,0:T(8,128)(2,1)} %copy-done.3) | copy-start | bytes 491524
  110.6 1.5 %copy-start.6 = (bf16[1,256,1,5,64]{4,1,3,2,0:T(8,128)(2,1)S(1)}, bf16[1,256,1,5,64]{4,1,3,2,0:T(8,128)(2,1)}, u32[]{:S(2)}) copy-start(bf16[1,256,1,5,64]{4,1,3,2,0:T(8,128)(2,1)} %copy-done.5) | copy-start | bytes 491524
Sparse Core Ops, SparseCore 0:
  9.8 42.2 all-gather.1
  91.2 33.7 reduce-scatter.1
where the time goes:
time: 134 us; the launch traced here: 133 us
  matrix products  55.1 us (41%)
  blocking collectives  33.9 us (25%)
  between operations  15.1 us (11%)
  local copies, waits for them, and re-layouts  11.4 us (9%)
  waiting for transfers between devices  11 us (8%)
  other arithmetic  6.39 us (5%)
    all_gather x1, blocking collectives, local(): lax.all_gather(keys_prompt, 'roll', axis=0, tiled=True)  17.7 us
    dot_general x12, matrix products, inner_dot(): lax.dot_general(left, right, (((1,), (1,)), ((), ())), preferred_element_...  17.3 us
    all_gather x1, blocking collectives, local(): lax.all_gather(values_prompt, 'roll', axis=0, tiled=True)  16.1 us
    dot_general x4, matrix products, query_step(): jnp.dot(score_grad, blocks[0], preferred_element_type=jnp.float32)  11.5 us
    reduce_scatter x1, waiting for transfers between devices, local(): lax.psum_scatter(jnp.stack(pieces, axis=1).astype(jnp.bfloat16), 'roll',...  10.2 us
    dot_general x8, matrix products, outer_sum(): lax.dot_general(left, right, (((0,), (0,)), ((), ())), preferred_element_...  9.5 us
    dot_general x4, matrix products, output_step(): jnp.dot(attn_probs, blocks[1], preferred_element_type=jnp.float32)  7.7 us
    dot_general x1, matrix products, local(): jnp.einsum('rsc,ghdc->rsghd', lax.all_gather(out_grad, 'kvh', axis=1, til...  5.89 us
  transfers between devices with their start and end apart: 2, of which 1 were waited for; matrix products, arithmetic and copies ran while one was open for 34% of the time, Pallas kernels for 0%

commit v1 on v0

--- a/solution.py
+++ b/solution.py
@@ -84,7 +84,9 @@
         preferred_element_type=jnp.float32,
     ).astype(jnp.bfloat16)
     cached_keys, cached_values = (
-        lax.all_gather(keys_prompt, "roll", axis=0, tiled=True),
+        jnp.concatenate(
+            lax.all_to_all(jnp.stack([keys_prompt] * lax.axis_size("roll")), "roll", 0, 0), axis=0
+        ),
         lax.all_gather(values_prompt, "roll", axis=0, tiled=True),
     )
     positions = prompt_total + offsets[:, None] + jnp.arange(seq_len, dtype=jnp.int32)[None, :]

time: 134 us -> 126 us (0.940)
  blocking collectives: 33.9 us -> 16.6 us
  starting transfers between devices: 0.08 us -> 6.43 us
  local copies, waits for them, and re-layouts: 11.4 us -> 13.1 us
    all_gather x1 -> x0, blocking collectives: 17.7 us -> none  [local(): lax.all_gather(keys_prompt, 'roll', axis=0, tiled=True)]
    all_to_all x0 -> x1, starting transfers between devices: none -> 6.35 us  [local(): lax.all_to_all(jnp.stack([keys_prompt] * lax.axis_size('roll')), 'roll',...]
    another operation x2 -> x3, local copies, waits for them, and re-layouts: 0.48 us -> 2.24 us  [the longest x1 1.76 us: local(): jnp.stack([keys_prompt] * lax.axis_size('roll'))]
    all_gather x1, waiting for transfers between devices: 0.02 us -> 1.57 us  [local(): lax.all_gather(out_grad, 'kvh', axis=1, tiled=True)]
    unnamed x32 -> x36, local copies, waits for them, and re-layouts: 3.82 us -> 3.83 us
  transfers between devices with their start and end apart: 2 -> 3, of which waited for: 1 -> 2; matrix products, arithmetic and copies ran while one was open for 34% -> 37% of each run, Pallas kernels for 0% -> 0%
where the time goes in v1:
time: 126 us; the launch traced here: 125 us
  matrix products  55 us (44%)
  blocking collectives  16.6 us (13%)
  between operations  15.1 us (12%)
  local copies, waits for them, and re-layouts  13.1 us (10%)
  waiting for transfers between devices  11.5 us (9%)
  starting transfers between devices  6.43 us (5%)
  other arithmetic  6.37 us (5%)
    dot_general x12, matrix products, inner_dot(): lax.dot_general(left, right, (((1,), (1,)), ((), ())), preferred_element_...  17.3 us
    all_gather x1, blocking collectives, local(): lax.all_gather(values_prompt, 'roll', axis=0, tiled=True)  16.6 us
    dot_general x4, matrix products, query_step(): jnp.dot(score_grad, blocks[0], preferred_element_type=jnp.float32)  11.5 us
    dot_general x8, matrix products, outer_sum(): lax.dot_general(left, right, (((0,), (0,)), ((), ())), preferred_element_...  9.53 us
    reduce_scatter x1, waiting for transfers between devices, local(): lax.psum_scatter(jnp.stack(pieces, axis=1).astype(jnp.bfloat16), 'roll',...  9.22 us
    dot_general x4, matrix products, output_step(): jnp.dot(attn_probs, blocks[1], preferred_element_type=jnp.float32)  7.67 us
    all_to_all x1, starting transfers between devices, local(): lax.all_to_all(jnp.stack([keys_prompt] * lax.axis_size('roll')), 'roll',...  6.35 us
    dot_general x1, matrix products, local(): jnp.einsum('rsc,ghdc->rsghd', lax.all_gather(out_grad, 'kvh', axis=1, til...  5.89 us
  transfers between devices with their start and end apart: 3, of which 2 were waited for; matrix products, arithmetic and copies ran while one was open for 37% of the time, Pallas kernels for 0%

profile of v1, /device:TPU:0, one launch (start us, length us, event | category | flops | bytes accessed | tf_op | source)
XLA Modules:
  0.0 124.8 jit_solution(7360948401987355139)
XLA Ops:
  7.2 1.8 %stack.10 = bf16[8,256,1,128]{3,1,2,0:T(8,128)(2,1)} broadcast(bf16[256,128]{1,0:T(8,128)(2,1)} %bitcast.161), dimensions={1,3} | broadcast | bytes 589824 | tf_op jit(solution)/shard_map/stack | solution.py:88
  8.9 6.4 %all-to-all-start = ((bf16[8,256,1,128]{3,1,2,0:T(8,128)(2,1)}), bf16[8,256,1,128]{3,1,2,0:T(8,128)(2,1)}, u32[]{:S(2)}, u32[]{:S(2)}) async-start(bf16[8,256,1,128]{3,1,2,0:T(8,128)(2,1)} %stack.10), calls=%async_computation | async-start | bytes 1048576 | tf_op jit(solution)/shard_map/all_to_all | solution.py:88
  22.6 16.6 %all_gather.6 = bf16[2048,1,128]{2,0,1:T(8,128)(2,1)} all-gather(bf16[256,1,128]{2,0,1:T(8,128)(2,1)S(1)} %copy-done.12), channel_id=1, replica_groups=mesh['roll'=8,'kvh'=4] {'roll'}, dimensions={0}, use_global_device_ids=true | all-gather | bytes 589824 | tf_op jit(solution)/shard_map/all_gather | solution.py:90
  39.5 7.7 %while.43 = (s32[]{:T(128)}, f32[1280]{0:T(1024)S(1)}, f32[1280]{0:T(1024)S(1)}, bf16[4,512,128]{2,1,0:T(8,128)(2,1)}, bf16[1280,128]{1,0:T(8,128)(2,1)S(1)}, /*index=5*/s32[]{:T(128)}) while((s32[]{:T(128)}, f32[1280]{0:T(1024)S(1)}, f32[1280]{0:T(1024)S(1)}, bf16[4,512,128]{2,1,0:T(8,128)(2,1)}, bf16[1280,128]{1,0:T(8,128)(2,1)S(1)}, ...), condition=%wide.region_5.6_spmd, body=%wide.region_2.5_spmd.sunk | while | flops 170396160 | bytes 5768273 | solution.py:129
  49.6 7.7 %while.44 = (s32[]{:T(128)}, f32[1280,128]{1,0:T(8,128)S(1)}, bf16[4,512,128]{2,1,0:T(8,128)(2,1)}, bf16[1280,128]{1,0:T(8,128)(2,1)S(1)}, f32[1280]{0:T(1024)S(1)}, /*index=5*/bf16[4,512,128]{2,1,0:T(8,128)(2,1)}, s32[]{:T(128)}) while((s32[]{:T(128)}, f32[1280,128]{1,0:T(8,128)S(1)}, bf16[4,512,128]{2,1,0:T(8,128)(2,1)}, ...), condition=%wide.region_7.8_spmd, body=%wide.region_6.7_spmd.sunk | while | flops 337674240 | bytes 1906773 | solution.py:147
  49.6 1.9 %convolution_add_fusion.5 = f32[1280,128]{1,0:T(8,128)S(1)} fusion(f32[1280,128]{1,0:T(8,128)S(1)} %get-tuple-element.468, bf16[1280,128]{1,0:T(8,128)(2,1)S(1)} %get-tuple-element.477, f32[1280]{0:T(1024)S(1)} %get-tuple-element.478, bf16[4,512,128]{2,1,0:T(8,128)(2,1)} %get-tuple-element.479, s32[]{:T(128)S(6)} %copy.87, ...), kind=kOutput, calls=%fused_computation.10.clone.1 | convolution fusion | flops 337674240 | bytes 1906688 | tf_op jit(solution)/shard_map/while/body/eval_jaxpr/dot_general | solution.py:143
  51.6 1.9 %convolution_add_fusion.5 = f32[1280,128]{1,0:T(8,128)S(1)} fusion(f32[1280,128]{1,0:T(8,128)S(1)} %get-tuple-element.468, bf16[1280,128]{1,0:T(8,128)(2,1)S(1)} %get-tuple-element.477, f32[1280]{0:T(1024)S(1)} %get-tuple-element.478, bf16[4,512,128]{2,1,0:T(8,128)(2,1)} %get-tuple-element.479, s32[]{:T(128)S(6)} %copy.87, ...), kind=kOutput, calls=%fused_computation.10.clone.1 | convolution fusion | flops 337674240 | bytes 1906688 | tf_op jit(solution)/shard_map/while/body/eval_jaxpr/dot_general | solution.py:143
  53.5 1.9 %convolution_add_fusion.5 = f32[1280,128]{1,0:T(8,128)S(1)} fusion(f32[1280,128]{1,0:T(8,128)S(1)} %get-tuple-element.468, bf16[1280,128]{1,0:T(8,128)(2,1)S(1)} %get-tuple-element.477, f32[1280]{0:T(1024)S(1)} %get-tuple-element.478, bf16[4,512,128]{2,1,0:T(8,128)(2,1)} %get-tuple-element.479, s32[]{:T(128)S(6)} %copy.87, ...), kind=kOutput, calls=%fused_computation.10.clone.1 | convolution fusion | flops 337674240 | bytes 1906688 | tf_op jit(solution)/shard_map/while/body/eval_jaxpr/dot_general | solution.py:143
  55.5 1.9 %convolution_add_fusion.5 = f32[1280,128]{1,0:T(8,128)S(1)} fusion(f32[1280,128]{1,0:T(8,128)S(1)} %get-tuple-element.468, bf16[1280,128]{1,0:T(8,128)(2,1)S(1)} %get-tuple-element.477, f32[1280]{0:T(1024)S(1)} %get-tuple-element.478, bf16[4,512,128]{2,1,0:T(8,128)(2,1)} %get-tuple-element.479, s32[]{:T(128)S(6)} %copy.87, ...), kind=kOutput, calls=%fused_computation.10.clone.1 | convolution fusion | flops 337674240 | bytes 1906688 | tf_op jit(solution)/shard_map/while/body/eval_jaxpr/dot_general | solution.py:143
  57.4 1.6 %all-gather.2.cloned.1.call-done = bf16[1,256,5120]{2,1,0:T(8,128)(2,1)} async-done(((bf16[1,64,5120]{2,1,0:T(8,128)(2,1)}), bf16[1,256,5120]{2,1,0:T(8,128)(2,1)}) %all-gather.2.cloned.1.call-update) | async-done | bytes 2621456 | tf_op jit(solution)/shard_map/all_gather | solution.py:82
  58.9 5.9 %fusion.67 = bf16[256,5,128]{2,0,1:T(8,128)(2,1)S(1)} fusion(bf16[1,5,128,5120]{3,2,1,0:T(8,128)(2,1)} %param.17, bf16[1,256,5120]{2,1,0:T(8,128)(2,1)} %all-gather.2.cloned.1.call-done), kind=kOutput, calls=%fused_computation.75 | convolution fusion | flops 1677885440 | bytes 9502720 | tf_op jit(solution)/shard_map/rsc,ghdc->rsghd/dot_general | solution.py:80
  66.8 15.8 %while.45 = (s32[]{:T(128)}, bf16[4,512,2,128]{3,1,2,0:T(8,128)(2,1)S(1)}, bf16[4,512,128]{2,1,0:T(8,128)(2,1)}, bf16[1280,128]{1,0:T(8,128)(2,1)S(1)}, f32[1280...) while((s32[]{:T(128)}, ...), condition=%wide.region_12.13_spmd, body=%wide.region_11.12_spmd.sunk | while | flops 676855808 | bytes 6301809 | solution.py:68
  68.8 1.9 %fusion.153 = bf16[512,1,128]{2,0,1:T(8,128)(2,1)S(1)} fusion(bf16[1280,128]{1,0:T(8,128)(2,1)S(1)} %get-tuple-element.532, bf16[1280,128]{1,0:T(8,128)(2,1)S(1)} %get-tuple-element.535, bf16[512,1280]{1,0:T(8,128)(2,1)S(1)} %fusion.152, f32[1280]{0:T(1024)S(1)} %get-tuple-element.536, bf16[4,512,128]{2,1,0:T(8,128)(2,1)} %get-tuple-element.534, ...), kind=kOutput, calls=%fused_computation.30.clone.1 | convolution fusion | flops 338821120 | bytes 2233348 | tf_op jit(solution)/shard_map/while/body/eval_jaxpr/dot_general | solution.py:37
  70.7 1.5 %fusion.152 = bf16[512,1280]{1,0:T(8,128)(2,1)S(1)} fusion(bf16[1280,128]{1,0:T(8,128)(2,1)S(1)} %get-tuple-element.532, f32[1280]{0:T(1024)S(1)} %get-tuple-element.533, bf16[4,512,128]{2,1,0:T(8,128)(2,1)} %get-tuple-element.531, s32[]{:T(128)S(6)} %copy.99), kind=kOutput, calls=%fused_computation.25.clone.1 | convolution fusion | flops 169738240 | bytes 1774596 | tf_op jit(solution)/shard_map/while/body/eval_jaxpr/dot_general | solution.py:31
  72.7 1.9 %fusion.153 = bf16[512,1,128]{2,0,1:T(8,128)(2,1)S(1)} fusion(bf16[1280,128]{1,0:T(8,128)(2,1)S(1)} %get-tuple-element.532, bf16[1280,128]{1,0:T(8,128)(2,1)S(1)} %get-tuple-element.535, bf16[512,1280]{1,0:T(8,128)(2,1)S(1)} %fusion.152, f32[1280]{0:T(1024)S(1)} %get-tuple-element.536, bf16[4,512,128]{2,1,0:T(8,128)(2,1)} %get-tuple-element.534, ...), kind=kOutput, calls=%fused_computation.30.clone.1 | convolution fusion | flops 338821120 | bytes 2233348 | tf_op jit(solution)/shard_map/while/body/eval_jaxpr/dot_general | solution.py:37
  76.7 1.9 %fusion.153 = bf16[512,1,128]{2,0,1:T(8,128)(2,1)S(1)} fusion(bf16[1280,128]{1,0:T(8,128)(2,1)S(1)} %get-tuple-element.532, bf16[1280,128]{1,0:T(8,128)(2,1)S(1)} %get-tuple-element.535, bf16[512,1280]{1,0:T(8,128)(2,1)S(1)} %fusion.152, f32[1280]{0:T(1024)S(1)} %get-tuple-element.536, bf16[4,512,128]{2,1,0:T(8,128)(2,1)} %get-tuple-element.534, ...), kind=kOutput, calls=%fused_computation.30.clone.1 | convolution fusion | flops 338821120 | bytes 2233348 | tf_op jit(solution)/shard_map/while/body/eval_jaxpr/dot_general | solution.py:37
  80.6 1.9 %fusion.153 = bf16[512,1,128]{2,0,1:T(8,128)(2,1)S(1)} fusion(bf16[1280,128]{1,0:T(8,128)(2,1)S(1)} %get-tuple-element.532, bf16[1280,128]{1,0:T(8,128)(2,1)S(1)} %get-tuple-element.535, bf16[512,1280]{1,0:T(8,128)(2,1)S(1)} %fusion.152, f32[1280]{0:T(1024)S(1)} %get-tuple-element.536, bf16[4,512,128]{2,1,0:T(8,128)(2,1)} %get-tuple-element.534, ...), kind=kOutput, calls=%fused_computation.30.clone.1 | convolution fusion | flops 338821120 | bytes 2233348 | tf_op jit(solution)/shard_map/while/body/eval_jaxpr/dot_general | solution.py:37
  83.6 17.2 %while.46 = (s32[]{:T(128)}, f32[1280,128]{1,0:T(8,128)}, bf16[4,512,128]{2,1,0:T(8,128)(2,1)}, bf16[1280,128]{1,0:T(8,128)(2,1)S(1)}, f32[1280]{0:T(1024)S(1)},...) while((s32[]{:T(128)}, f32[1280,128]{1,0:T(8,128)}, ...), condition=%wide.region_10.11_spmd.clone, body=%wide.region_9.10_spmd.clone.sunk | while | flops 508887040 | bytes 7614074 | solution.py:176
  85.1 2.7 %convolution_add_fusion.6 = f32[1280,128]{1,0:T(8,128)} fusion(f32[512,1280]{1,0:T(8,128)S(1)} %fusion.160, bf16[1280,128]{1,0:T(8,128)(2,1)S(1)} %get-tuple-element.507, f32[1280]{0:T(1024)S(1)} %get-tuple-element.508, f32[1280,128]{1,0:T(8,128)} %get-tuple-element.492, pred[]{:T(512)S(6)} %compare.3, bf16[4,512,128]{2,1,0:T(8,128)(2,1)} %get-tuple-element.506, ...), kind=kOutput, calls=%fused_computation.50.clone.1 | convolution fusion | flops 338493440 | bytes 4528640 | tf_op jit(solution)/shard_map/while/body/eval_jaxpr/dot_general | solution.py:172
  89.2 2.9 %convolution_add_fusion.6 = f32[1280,128]{1,0:T(8,128)} fusion(f32[512,1280]{1,0:T(8,128)S(1)} %fusion.160, bf16[1280,128]{1,0:T(8,128)(2,1)S(1)} %get-tuple-element.507, f32[1280]{0:T(1024)S(1)} %get-tuple-element.508, f32[1280,128]{1,0:T(8,128)} %get-tuple-element.492, pred[]{:T(512)S(6)} %compare.3, bf16[4,512,128]{2,1,0:T(8,128)(2,1)} %get-tuple-element.506, ...), kind=kOutput, calls=%fused_computation.50.clone.1 | convolution fusion | flops 338493440 | bytes 4528640 | tf_op jit(solution)/shard_map/while/body/eval_jaxpr/dot_general | solution.py:172
  93.6 2.9 %convolution_add_fusion.6 = f32[1280,128]{1,0:T(8,128)} fusion(f32[512,1280]{1,0:T(8,128)S(1)} %fusion.160, bf16[1280,128]{1,0:T(8,128)(2,1)S(1)} %get-tuple-element.507, f32[1280]{0:T(1024)S(1)} %get-tuple-element.508, f32[1280,128]{1,0:T(8,128)} %get-tuple-element.492, pred[]{:T(512)S(6)} %compare.3, bf16[4,512,128]{2,1,0:T(8,128)(2,1)} %get-tuple-element.506, ...), kind=kOutput, calls=%fused_computation.50.clone.1 | convolution fusion | flops 338493440 | bytes 4528640 | tf_op jit(solution)/shard_map/while/body/eval_jaxpr/dot_general | solution.py:172
  97.9 2.9 %convolution_add_fusion.6 = f32[1280,128]{1,0:T(8,128)} fusion(f32[512,1280]{1,0:T(8,128)S(1)} %fusion.160, bf16[1280,128]{1,0:T(8,128)(2,1)S(1)} %get-tuple-element.507, f32[1280]{0:T(1024)S(1)} %get-tuple-element.508, f32[1280,128]{1,0:T(8,128)} %get-tuple-element.492, pred[]{:T(512)S(6)} %compare.3, bf16[4,512,128]{2,1,0:T(8,128)(2,1)} %get-tuple-element.506, ...), kind=kOutput, calls=%fused_computation.50.clone.1 | convolution fusion | flops 338493440 | bytes 4528640 | tf_op jit(solution)/shard_map/while/body/eval_jaxpr/dot_general | solution.py:172
  107.2 9.2 %reduce-scatter.2.cloned.1.call-done = bf16[256,1,2,128]{3,0,2,1:T(8,128)(2,1)} async-done(((bf16[2048,1,2,128]{3,0,2,1:T(8,128)(2,1)}), bf16[256,1,2,128]{3,0,2,1:T(8,128)(2,1)}) %reduce-scatter.2.cloned.1.call-update) | async-done | bytes 131088 | tf_op jit(solution)/shard_map/reduce_scatter | solution.py:187
  116.4 1.5 %slice_bitcast_fusion = (bf16[256,1,128]{2,0,1:T(8,128)(2,1)}, bf16[256,1,128]{2,0,1:T(8,128)(2,1)}) fusion(bf16[256,1,2,128]{3,0,2,1:T(8,128)(2,1)} %reduce-scatter.2.cloned.1.call-done), kind=kLoop, calls=%fused_computation.113 | loop fusion | bytes 262144 | tf_op jit(solution)/shard_map/convert_element_type | solution.py:198
  (122 shorter events, 38.0 us)
Async XLA Ops:
  7.2 42.1 %copy-start = (bf16[1,256,1,128]{3,1,2,0:T(8,128)(2,1)S(1)}, bf16[1,256,1,128]{3,1,2,0:T(8,128)(2,1)}, u32[]{:S(2)}) copy-start(bf16[1,256,1,128]{3,1,2,0:T(8,128)(2,1)} %param.20) | copy-start | bytes 196612
  7.2 11.8 %copy-start.11 = (bf16[1,256,1,128]{3,1,2,0:T(8,128)(2,1)S(1)}, bf16[1,256,1,128]{3,1,2,0:T(8,128)(2,1)}, u32[]{:S(2)}) copy-start(bf16[1,256,1,128]{3,1,2,0:T(8,128)(2,1)} %param.19) | copy-start | bytes 196612
  8.9 30.5 %all-to-all-start = ((bf16[8,256,1,128]{3,1,2,0:T(8,128)(2,1)}), bf16[8,256,1,128]{3,1,2,0:T(8,128)(2,1)}, u32[]{:S(2)}, u32[]{:S(2)}) async-start(bf16[8,256,1,128]{3,1,2,0:T(8,128)(2,1)} %stack.10), calls=%async_computation | async-start | bytes 1048576 | tf_op jit(solution)/shard_map/all_to_all | solution.py:88
  15.3 43.6 %all-gather.2.cloned.1.call-start = ((), (), s32[]{:S(2)}) async-start(), calls=%async_computation.2 | async-start | bytes 3276800 | tf_op jit(solution)/shard_map/all_gather | solution.py:82
  16.0 100.4 %reduce-scatter.2.cloned.1.call-start = ((), (), s32[]{:S(2)}) async-start(), calls=%async_computation.3 | async-start | bytes 1179648 | tf_op jit(solution)/shard_map/reduce_scatter | solution.py:187
  16.1 2.9 %copy-start.15 = (f32[64]{0:T(128)}, f32[64]{0:T(128)S(1)}, u32[]{:S(2)}) copy-start(f32[64]{0:T(128)S(1)} %negate_power_fusion) | copy-start | bytes 772
  17.8 1.2 copy-start.13
  19.9 1.6 %copy-start.3 = (bf16[1,256,1,5,64]{4,1,3,2,0:T(8,128)(2,1)}, bf16[1,256,1,5,64]{4,1,3,2,0:T(8,128)(2,1)S(1)}, u32[]{:S(2)}) copy-start(bf16[1,256,1,5,64]{4,1,3,2,0:T(8,128)(2,1)S(1)} %get-tuple-element.257) | copy-start | bytes 491524
  19.9 1.6 %copy-start.5 = (bf16[1,256,1,5,64]{4,1,3,2,0:T(8,128)(2,1)}, bf16[1,256,1,5,64]{4,1,3,2,0:T(8,128)(2,1)S(1)}, u32[]{:S(2)}) copy-start(bf16[1,256,1,5,64]{4,1,3,2,0:T(8,128)(2,1)S(1)} %get-tuple-element.258) | copy-start | bytes 491524
  20.7 2.0 %copy-start.12 = (bf16[256,1,128]{2,0,1:T(8,128)(2,1)S(1)}, bf16[256,1,128]{2,0,1:T(8,128)(2,1)}, u32[]{:S(2)}) copy-start(bf16[256,1,128]{2,0,1:T(8,128)(2,1)} %param.22) | copy-start | bytes 196612
  47.8 0.9 copy-start.1
  64.8 0.7 copy-start.7
  65.6 1.2 copy-start.9
  100.9 1.9 %copy-start.2 = (bf16[256,5,256]{2,0,1:T(8,128)(2,1)S(1)}, bf16[256,5,256]{2,0,1:T(8,128)(2,1)}, u32[]{:S(2)}) copy-start(bf16[256,5,256]{2,0,1:T(8,128)(2,1)} %copy-done.1) | copy-start | bytes 1966084
  100.9 1.9 %copy-start.8 = (bf16[256,5,128]{2,0,1:T(8,128)(2,1)S(1)}, bf16[256,5,128]{2,0,1:T(8,128)(2,1)}, u32[]{:S(2)}) copy-start(bf16[256,5,128]{2,0,1:T(8,128)(2,1)} %copy-done.7) | copy-start | bytes 983044
  102.3 1.3 %copy-start.10 = (f32[256,64]{0,1:T(8,128)S(1)}, f32[256,64]{0,1:T(8,128)}, u32[]{:S(2)}) copy-start(f32[256,64]{0,1:T(8,128)} %get-tuple-element.267) | copy-start | bytes 196612
  103.1 1.5 %copy-start.4 = (bf16[1,256,1,5,64]{4,1,3,2,0:T(8,128)(2,1)S(1)}, bf16[1,256,1,5,64]{4,1,3,2,0:T(8,128)(2,1)}, u32[]{:S(2)}) copy-start(bf16[1,256,1,5,64]{4,1,3,2,0:T(8,128)(2,1)} %copy-done.3) | copy-start | bytes 491524
  103.1 1.5 %copy-start.6 = (bf16[1,256,1,5,64]{4,1,3,2,0:T(8,128)(2,1)S(1)}, bf16[1,256,1,5,64]{4,1,3,2,0:T(8,128)(2,1)}, u32[]{:S(2)}) copy-start(bf16[1,256,1,5,64]{4,1,3,2,0:T(8,128)(2,1)} %copy-done.5) | copy-start | bytes 491524
  103.1 2.0 %copy-start.14 = (f32[256]{0:T(256)S(1)}, f32[256]{0:T(256)}, u32[]{:S(2)}) copy-start(f32[256]{0:T(256)} %copy-done.13) | copy-start | bytes 3076
  103.2 2.0 %copy-start.16 = (f32[64]{0:T(128)S(1)}, f32[64]{0:T(128)}, u32[]{:S(2)}) copy-start(f32[64]{0:T(128)} %copy-done.15) | copy-start | bytes 772
Sparse Core Ops, SparseCore 0:
  17.9 40.9 all-gather.1
  83.8 32.6 reduce-scatter.1
